TPU v7x, 32 devices: a whole 2x2x4 slice. The times are simulated.
32 devices in a mesh: rep: 2 (over x), grp: 8 (over z, y), loc: 2 (over core).
Axes of the slice: x: 2, y: 2, z: 4, core: 2. Of those that a mesh axis runs over, the one named last changes fastest.
Arguments:
- tokens: bfloat16 [4096, 3584], P(('rep', 'grp', 'loc')), parts along dimension 0, may hold values from -6 to 6
- norm_gain: float32 [3584], replicated, may hold values from 0.5 to 1.5
- gate_weight: bfloat16 [8, 3584, 1024], P('grp', 'loc'), may hold values from -0.09375 to 0.09375
- up_weight: bfloat16 [8, 3584, 1024], P('grp', 'loc'), may hold values from -0.09375 to 0.09375
- down_weight: bfloat16 [8, 1024, 3584], P('grp', None, 'loc'), may hold values from -0.1875 to 0.1875
- expert_ids: int32 [4096, 4], P(('rep', 'grp', 'loc')), parts along dimension 0, may hold values from 0 to 7, as said below
- numerators: int32 [4096, 4], P(('rep', 'grp', 'loc')), parts along dimension 0, may hold values from 1 to 128
Outputs:
- moe_out: bfloat16 [4096, 3584], P(('rep', 'grp', 'loc')), parts along dimension 0
There are 2 independent parts, one for each index of `rep`. A program takes and returns all parts, laid end to end along the dimension named above; an argument that names none is the same for every part. Nothing has to cross between parts.
Inputs may be any that keep to these rules, and one draw needn't show every extreme that they name: `expert_ids`: expert e lies in group e // 1. Each token names 4 different experts, one in each of four different groups. In each aligned block of 128 tokens every group is named by exactly half of the tokens, no expert is named by more than 64 tokens, and some expert is named by exactly 64; some experts are named by 64 tokens of every block.
All inputs are finite; a program needn't handle non-finite values.
Results may differ from a plain program's by a relative error of at most 0.015.
Values may be sent and summed in bfloat16 or wider, within the bound.
No kernel may reach another device: no remote copies, remote signals or barrier semaphores. Data moves between devices by JAX's collectives and lax.ppermute only.
A program may use at most 64 MiB of HBM per device.

v0:
```python
import jax
import jax.numpy as jnp
from jax import lax
from jax.sharding import PartitionSpec as P


def local(tokens, norm_gain, gate_weight, up_weight, down_weight, expert_ids, numerators):
    tok_count, width = tokens.shape
    chosen = expert_ids.shape[1]
    experts = lax.axis_size("grp")
    halves = lax.axis_size("loc")
    half_width = width // halves
    capacity = tok_count // 2 - experts // 32 * (23 * tok_count // 64)
    values = tokens.astype(jnp.float32)
    norm_scale = lax.rsqrt(jnp.mean(values * values, axis=-1, keepdims=True) + 1e-06)
    normed = (values * norm_scale * norm_gain).astype(jnp.bfloat16)
    flat_ids = expert_ids.reshape(-1)
    onehot = (flat_ids[:, None] == jnp.arange(experts, dtype=jnp.int32)[None, :]).astype(jnp.int32)
    slot_rank = jnp.sum((jnp.cumsum(onehot, axis=0) - 1) * onehot, axis=1)
    target = (flat_ids * capacity + slot_rank).reshape(tok_count, chosen)
    placed = (
        target[:, :, None] == jnp.arange(experts * capacity, dtype=jnp.int32)[None, None, :]
    ).astype(jnp.float32)
    select = jnp.sum(placed, axis=1).astype(jnp.bfloat16).reshape(tok_count, experts, capacity)
    weights = numerators.astype(jnp.float32) / 128.0
    combine = (
        jnp.sum(placed * weights[:, :, None], axis=1)
        .astype(jnp.bfloat16)
        .reshape(tok_count, experts, capacity)
    )
    feature_halves = normed.reshape(tok_count, halves, half_width)
    outgoing = jnp.einsum(
        "tec,thf->ehcf", select, feature_halves, preferred_element_type=jnp.float32
    ).astype(jnp.bfloat16)
    arrived = lax.all_to_all(
        outgoing.reshape(experts * halves, capacity, half_width),
        ("grp", "loc"),
        split_axis=0,
        concat_axis=0,
        tiled=True,
    )
    expert_input = arrived.reshape(-1, half_width)
    gate_part = jnp.dot(expert_input, gate_weight[0], preferred_element_type=jnp.float32)
    up_part = jnp.dot(expert_input, up_weight[0], preferred_element_type=jnp.float32)
    down_local = down_weight[0]
    gate_sum, up_sum = (
        lax.psum(gate_part.astype(jnp.bfloat16), "loc").astype(jnp.float32),
        lax.psum(up_part.astype(jnp.bfloat16), "loc").astype(jnp.float32),
    )
    hidden_all = (jax.nn.silu(gate_sum) * up_sum).astype(jnp.bfloat16)
    expert_out = jnp.dot(hidden_all, down_local, preferred_element_type=jnp.float32)
    expert_out = expert_out.astype(jnp.bfloat16)
    returned = lax.all_to_all(
        expert_out.reshape(experts * halves, capacity, half_width),
        ("grp", "loc"),
        split_axis=0,
        concat_axis=0,
        tiled=True,
    ).reshape(experts, halves, capacity, half_width)
    mixed = jnp.einsum("tec,ehcf->thf", combine, returned, preferred_element_type=jnp.float32)
    return mixed.reshape(tok_count, width).astype(jnp.bfloat16)


def solution(mesh):
    in_specs = (
        P(("rep", "grp", "loc"), None),
        P(),
        P("grp", "loc", None),
        P("grp", "loc", None),
        P("grp", None, "loc"),
        P(("rep", "grp", "loc"), None),
        P(("rep", "grp", "loc"), None),
    )
    out_specs = P(("rep", "grp", "loc"), None)
    return jax.shard_map(local, mesh=mesh, in_specs=in_specs, out_specs=out_specs, check_vma=False)
```

profile of v0, /device:TPU:13, one launch (start us, length us, event | category | flops | bytes accessed | tf_op | source)
XLA Modules:
  0.0 266.5 jit_solution(13242521310978403542)
XLA Ops:
  6.5 0.8 copy.40
  7.3 0.1 eq.42
  7.4 0.1 eq.38
  7.5 1.4 fusion.20
  9.0 0.7 convert_multiply_fusion.3
  9.7 1.1 reduce-window.6
  10.8 0.2 slice_reduce_fusion
  11.1 0.1 fusion.24
  11.2 0.1 reduce_sum.39
  11.3 0.1 copy.42
  11.4 0.7 multiply_add_fusion
  12.1 0.2 convert_reduce_fusion
  12.3 0.1 copy.44
  12.4 1.5 fusion.22
  13.9 0.2 reshape.66
  14.1 1.1 fusion.11
  15.2 0.4 copy.46
  15.6 0.0 copy-start
  15.6 87.6 %all_to_all.10 = bf16[16,64,1792]{2,1,0:T(8,128)(2,1)S(1)} all-to-all(bf16[16,64,1792]{2,1,0:T(8,128)(2,1)S(1)} %bitcast.44), channel_id=1, replica_groups=mesh['rep'=2,'grp'=8,'loc'=2] {'grp','loc'}, dimensions={0} | all-to-all | bytes 7340032 | tf_op jit(solution)/shard_map/all_to_all | solution.py:35
  103.2 0.0 copy-done
  103.2 5.2 %fusion.17 = bf16[1024,1024]{1,0:T(8,128)(2,1)} fusion(bf16[1024,1792]{1,0:T(8,128)(2,1)S(1)} %bitcast.48, bf16[1,1792,1024]{2,1,0:T(8,128)(2,1)S(1)} %copy-done), kind=kOutput, calls=%fused_computation.22 | convolution fusion | flops 3759144960 | bytes 9437184 | tf_op jit(solution)/shard_map/dot_general | solution.py:44
  108.4 0.0 copy-done.1
  108.4 5.2 %fusion.14 = bf16[1024,1024]{1,0:T(8,128)(2,1)} fusion(bf16[1024,1792]{1,0:T(8,128)(2,1)S(1)} %bitcast.49, bf16[1,1792,1024]{2,1,0:T(8,128)(2,1)S(1)} %copy-done.1), kind=kOutput, calls=%fused_computation.21 | convolution fusion | flops 3759144960 | bytes 9437184 | tf_op jit(solution)/shard_map/dot_general | solution.py:43
  113.6 0.0 all-reduce.3.cloned.1.call-update
  113.6 29.0 %all-reduce.3.cloned.1.call-done = (bf16[1024,1024]{1,0:T(8,128)(2,1)}, bf16[1024,1024]{1,0:T(8,128)(2,1)}) async-done(((bf16[1024,1024]{1,0:T(8,128)(2,1)}, bf16[1024,1024]{1,0:T(8,128)(2,1)}), (bf16[1024,1024]{1,0:T(8,128)(2,1)}, bf16[1024,1024]{1,0:T(8,128)(2,1)})) %all-reduce.3.cloned.1.call-update) | async-done | bytes 4194320 | tf_op jit(solution)/shard_map/psum | solution.py:48
  142.6 9.9 %convolution_convert_fusion.1 = bf16[1024,1792]{1,0:T(8,128)(2,1)} fusion(bf16[1,1024,1792]{2,1,0:T(8,128)(2,1)} %param.11, bf16[1024,1024]{1,0:T(8,128)(2,1)} %get-tuple-element.7, bf16[1024,1024]{1,0:T(8,128)(2,1)} %get-tuple-element.8), kind=kOutput, calls=%fused_computation.10 | convolution fusion | flops 3768320000 | bytes 11534336 | tf_op jit(solution)/shard_map/dot_general | solution.py:51
  152.5 5.9 %all-to-all-start.1 = ((bf16[16,64,1792]{2,1,0:T(8,128)(2,1)}), bf16[16,64,1792]{2,1,0:T(8,128)(2,1)}, u32[]{:S(2)}, u32[]{:S(2)}) async-start(bf16[16,64,1792]{2,1,0:T(8,128)(2,1)} %bitcast.47), calls=%async_computation.1 | async-start | bytes 7340032 | tf_op jit(solution)/shard_map/all_to_all | solution.py:53
  158.3 0.1 copy.43
  158.5 81.1 %all-to-all-done.1 = bf16[16,64,1792]{2,1,0:T(8,128)(2,1)} async-done(((bf16[16,64,1792]{2,1,0:T(8,128)(2,1)}), bf16[16,64,1792]{2,1,0:T(8,128)(2,1)}, u32[]{:S(2)}, u32[]{:S(2)}) %all-to-all-start.1) | async-done | bytes 3670048 | tf_op jit(solution)/shard_map/all_to_all | solution.py:53
  239.6 7.6 %copy.54 = bf16[8,2,64,1792]{3,1,2,0:T(2,128)(2,1)} copy(bf16[8,2,64,1792]{3,2,1,0:T(8,128)(2,1)} %bitcast.13) | data formatting | bytes 7340032 | tf_op jit(solution)/shard_map/reshape | solution.py:59
  247.2 8.8 %dot_general.24 = bf16[3584,64,8]{0,1,2:T(8,128)(2,1)} reshape(bf16[2,1792,64,8]{1,0,2,3:T(2,128)(2,1)} %bitcast.45) | data formatting | bytes 7340032 | tf_op jit(solution)/shard_map/tec,ehcf->thf/dot_general | solution.py:60
  256.1 3.6 %fusion = bf16[128,3584]{1,0:T(8,128)(2,1)} fusion(bf16[128,8,64]{0,2,1:T(8,128)(2,1)S(1)} %bitcast.51, bf16[3584,64,8]{0,1,2:T(8,128)(2,1)} %dot_general.24), kind=kOutput, calls=%fused_computation.3 | convolution fusion | flops 470220800 | bytes 4718592 | tf_op jit(solution)/shard_map/tec,ehcf->thf/dot_general | solution.py:60
  (6 shorter events, 0.1 us)
Async XLA Ops:
  6.5 136.1 %all-reduce.3.cloned.1.call-start = ((), (), s32[]{:S(2)}) async-start(), calls=%async_computation.2 | async-start | bytes 8388608 | tf_op jit(solution)/shard_map/psum | solution.py:48
  15.6 87.6 %copy-start = (bf16[1,1792,1024]{2,1,0:T(8,128)(2,1)S(1)}, bf16[1,1792,1024]{2,1,0:T(8,128)(2,1)}, u32[]{:S(2)}) copy-start(bf16[1,1792,1024]{2,1,0:T(8,128)(2,1)} %param.10) | copy-start | bytes 11010052
  103.2 5.2 %copy-start.1 = (bf16[1,1792,1024]{2,1,0:T(8,128)(2,1)S(1)}, bf16[1,1792,1024]{2,1,0:T(8,128)(2,1)}, u32[]{:S(2)}) copy-start(bf16[1,1792,1024]{2,1,0:T(8,128)(2,1)} %param.9) | copy-start | bytes 11010052
  152.5 87.1 %all-to-all-start.1 = ((bf16[16,64,1792]{2,1,0:T(8,128)(2,1)}), bf16[16,64,1792]{2,1,0:T(8,128)(2,1)}, u32[]{:S(2)}, u32[]{:S(2)}) async-start(bf16[16,64,1792]{2,1,0:T(8,128)(2,1)} %bitcast.47), calls=%async_computation.1 | async-start | bytes 7340032 | tf_op jit(solution)/shard_map/all_to_all | solution.py:53
Sparse Core Ops, SparseCore 0:
  113.7 28.8 all-reduce.2
where the time goes:
time: 267 us
  waiting for transfers between devices  110 us (41%)
  blocking collectives  87.6 us (33%)
  matrix products  25 us (9%)
  local copies, waits for them, and re-layouts  18.7 us (7%)
  between operations  13.5 us (5%)
  starting transfers between devices  5.89 us (2%)
  other arithmetic  5.83 us (2%)
    all_to_all x1, blocking collectives, local(): lax.all_to_all(outgoing.reshape(experts * halves, capacity, half_width),...  87.6 us
    all_to_all x1, waiting for transfers between devices, local(): lax.all_to_all(expert_out.reshape(experts * halves, capacity, half_width)...  81.1 us
    psum x1, waiting for transfers between devices, local(): lax.psum(up_part.astype(jnp.bfloat16), 'loc').astype(jnp.float32)  29 us
    dot_general x1, matrix products, local(): jnp.dot(hidden_all, down_local, preferred_element_type=jnp.float32)  9.86 us
    dot_general x1, local copies, waits for them, and re-layouts, local(): jnp.einsum('tec,ehcf->thf', combine, returned, preferred_element_type=jnp...  8.84 us
    reshape x1, local copies, waits for them, and re-layouts, local(): returned = lax.all_to_all(expert_out.reshape(experts * halves, capacity,...  7.65 us
    all_to_all x1, starting transfers between devices, local(): lax.all_to_all(expert_out.reshape(experts * halves, capacity, half_width)...  5.89 us
  transfers between devices with their start and end apart: 2, of which 2 were waited for; matrix products, arithmetic and copies ran while one was open for 0% of the time, Pallas kernels for 0%

commit v1 on v0

--- a/solution.py
+++ b/solution.py
@@ -43,9 +43,14 @@
     gate_part = jnp.dot(expert_input, gate_weight[0], preferred_element_type=jnp.float32)
     up_part = jnp.dot(expert_input, up_weight[0], preferred_element_type=jnp.float32)
     down_local = down_weight[0]
+
+    def tell_digits(local_values, group_axis):
+        next_value = jnp.sum(lax.all_gather(local_values, group_axis), 0)
+        return next_value
+
     gate_sum, up_sum = (
         lax.psum(gate_part.astype(jnp.bfloat16), "loc").astype(jnp.float32),
-        lax.psum(up_part.astype(jnp.bfloat16), "loc").astype(jnp.float32),
+        tell_digits(up_part.astype(jnp.bfloat16), "loc").astype(jnp.float32),
     )
     hidden_all = (jax.nn.silu(gate_sum) * up_sum).astype(jnp.bfloat16)
     expert_out = jnp.dot(hidden_all, down_local, preferred_element_type=jnp.float32)

time: 267 us -> 273 us (1.022)
  other arithmetic: 5.83 us -> 9.94 us
  waiting for transfers between devices: 110 us -> 107 us
    psum x1, waiting for transfers between devices: 29 us -> 20.7 us  [local(): lax.psum(gate_part.astype(jnp.bfloat16), 'loc').astype(jnp.float32)]
    all_gather x0 -> x1, waiting for transfers between devices: none -> 5.53 us  [tell_digits(): next_value = jnp.sum(lax.all_gather(local_values, group_axis), 0)]
    reduce_sum x0 -> x1, other arithmetic: none -> 4.11 us  [tell_digits(): next_value = jnp.sum(lax.all_gather(local_values, group_axis), 0)]
    dot_general x1, matrix products: 5.17 us -> 8.53 us  [local(): jnp.dot(expert_input, gate_weight[0], preferred_element_type=jnp.float32)]
  transfers between devices with their start and end apart: 2 -> 3, of which waited for: 2 -> 3; matrix products, arithmetic and copies ran while one was open for 0% -> 5% of each run, Pallas kernels for 0% -> 0%
where the time goes in v1:
time: 273 us
  waiting for transfers between devices  107 us (39%)
  blocking collectives  87.6 us (32%)
  matrix products  27.6 us (10%)
  local copies, waits for them, and re-layouts  20.5 us (8%)
  between operations  13.5 us (5%)
  other arithmetic  9.94 us (4%)
  starting transfers between devices  6.12 us (2%)
    all_to_all x1, blocking collectives, local(): lax.all_to_all(outgoing.reshape(experts * halves, capacity, half_width),...  87.6 us
    all_to_all x1, waiting for transfers between devices, local(): lax.all_to_all(expert_out.reshape(experts * halves, capacity, half_width)...  81.1 us
    psum x1, waiting for transfers between devices, local(): lax.psum(gate_part.astype(jnp.bfloat16), 'loc').astype(jnp.float32)  20.7 us
    dot_general x1, matrix products, local(): jnp.dot(hidden_all, down_local, preferred_element_type=jnp.float32)  9.23 us
    dot_general x1, local copies, waits for them, and re-layouts, local(): jnp.einsum('tec,ehcf->thf', combine, returned, preferred_element_type=jnp...  8.84 us
    dot_general x1, matrix products, local(): jnp.dot(expert_input, gate_weight[0], preferred_element_type=jnp.float32)  8.53 us
    reshape x1, local copies, waits for them, and re-layouts, local(): returned = lax.all_to_all(expert_out.reshape(experts * halves, capacity,...  7.65 us
    all_to_all x1, starting transfers between devices, local(): lax.all_to_all(expert_out.reshape(experts * halves, capacity, half_width)...  5.89 us
  transfers between devices with their start and end apart: 3, of which 3 were waited for; matrix products, arithmetic and copies ran while one was open for 5% of the time, Pallas kernels for 0%

profile of v1, /device:TPU:13, one launch (start us, length us, event | category | flops | bytes accessed | tf_op | source)
XLA Modules:
  0.0 272.6 jit_solution(12138564660163355068)
XLA Ops:
  6.5 0.8 copy.40
  7.3 0.1 eq.42
  7.4 0.1 eq.38
  7.5 1.4 fusion.20
  9.0 0.7 convert_multiply_fusion.3
  9.7 1.1 reduce-window.6
  10.8 0.2 slice_reduce_fusion
  11.1 0.1 fusion.24
  11.2 0.1 reduce_sum.51
  11.3 0.1 copy.42
  11.4 0.7 multiply_add_fusion
  12.1 0.2 convert_reduce_fusion
  12.3 0.1 copy.44
  12.4 1.5 fusion.22
  13.9 0.2 reshape.66
  14.1 1.1 fusion.11
  15.2 0.4 copy.46
  15.6 87.6 %all_to_all.10 = bf16[16,64,1792]{2,1,0:T(8,128)(2,1)S(1)} all-to-all(bf16[16,64,1792]{2,1,0:T(8,128)(2,1)S(1)} %bitcast.45), channel_id=1, replica_groups=mesh['rep'=2,'grp'=8,'loc'=2] {'grp','loc'}, dimensions={0} | all-to-all | bytes 7340032 | tf_op jit(solution)/shard_map/all_to_all | solution.py:35
  103.2 1.8 copy-done
  105.0 5.2 %fusion.17 = bf16[1024,1024]{1,0:T(8,128)(2,1)} fusion(bf16[1024,1792]{1,0:T(8,128)(2,1)S(1)} %bitcast.49, bf16[1,1792,1024]{2,1,0:T(8,128)(2,1)S(1)} %copy-done.1), kind=kOutput, calls=%fused_computation.22 | convolution fusion | flops 3759144960 | bytes 9437184 | tf_op jit(solution)/shard_map/dot_general | solution.py:44
  110.2 0.2 all-reduce.2.cloned.1.call-start
  110.4 8.5 %fusion.14 = bf16[1024,1024]{1,0:T(8,128)(2,1)} fusion(bf16[1024,1792]{1,0:T(8,128)(2,1)} %bitcast.50, bf16[1,1792,1024]{2,1,0:T(8,128)(2,1)} %param.9), kind=kOutput, calls=%fused_computation.21 | convolution fusion | flops 3759144960 | bytes 9437184 | tf_op jit(solution)/shard_map/dot_general | solution.py:43
  119.0 5.5 %all-gather.3.cloned.1.call-done = bf16[2048,1024]{1,0:T(8,128)(2,1)} async-done(((bf16[1024,1024]{1,0:T(8,128)(2,1)}), bf16[2048,1024]{1,0:T(8,128)(2,1)}) %all-gather.3.cloned.1.call-update) | async-done | bytes 4194320 | tf_op jit(solution)/shard_map/all_gather | solution.py:48
  124.5 4.1 %reduce_sum.55 = bf16[1024,1024]{1,0:T(8,128)(2,1)S(1)} reduce(bf16[2,1024,1024]{2,1,0:T(8,128)(2,1)} %bitcast.48, bf16[]{:T(256)} %constant.26.clone.1), dimensions={0}, to_apply=%region_7.8 | reduce | flops 1048576 | bytes 6291458 | tf_op jit(solution)/shard_map/reduce_sum | solution.py:48
  128.6 20.7 %all-reduce.2.cloned.1.call-done = bf16[1024,1024]{1,0:T(8,128)(2,1)} async-done(((bf16[1024,1024]{1,0:T(8,128)(2,1)}), bf16[1024,1024]{1,0:T(8,128)(2,1)}) %all-reduce.2.cloned.1.call-update) | async-done | bytes 2097168 | tf_op jit(solution)/shard_map/psum | solution.py:52
  149.3 9.2 %convolution_convert_fusion.1 = bf16[1024,1792]{1,0:T(8,128)(2,1)} fusion(bf16[1,1024,1792]{2,1,0:T(8,128)(2,1)} %param.11, bf16[1024,1024]{1,0:T(8,128)(2,1)S(1)} %reduce_sum.55, bf16[1024,1024]{1,0:T(8,128)(2,1)} %all-reduce.2.cloned.1.call-done), kind=kOutput, calls=%fused_computation.10 | convolution fusion | flops 3768320000 | bytes 11534336 | tf_op jit(solution)/shard_map/dot_general | solution.py:56
  158.6 5.9 %all-to-all-start.1 = ((bf16[16,64,1792]{2,1,0:T(8,128)(2,1)}), bf16[16,64,1792]{2,1,0:T(8,128)(2,1)}, u32[]{:S(2)}, u32[]{:S(2)}) async-start(bf16[16,64,1792]{2,1,0:T(8,128)(2,1)} %bitcast.51), calls=%async_computation.1 | async-start | bytes 7340032 | tf_op jit(solution)/shard_map/all_to_all | solution.py:58
  164.4 0.1 copy.43
  164.6 81.1 %all-to-all-done.1 = bf16[16,64,1792]{2,1,0:T(8,128)(2,1)} async-done(((bf16[16,64,1792]{2,1,0:T(8,128)(2,1)}), bf16[16,64,1792]{2,1,0:T(8,128)(2,1)}, u32[]{:S(2)}, u32[]{:S(2)}) %all-to-all-start.1) | async-done | bytes 3670048 | tf_op jit(solution)/shard_map/all_to_all | solution.py:58
  245.7 7.6 %copy.54 = bf16[8,2,64,1792]{3,1,2,0:T(2,128)(2,1)} copy(bf16[8,2,64,1792]{3,2,1,0:T(8,128)(2,1)} %bitcast.14) | data formatting | bytes 7340032 | tf_op jit(solution)/shard_map/reshape | solution.py:64
  253.3 8.8 %dot_general.24 = bf16[3584,64,8]{0,1,2:T(8,128)(2,1)} reshape(bf16[2,1792,64,8]{1,0,2,3:T(2,128)(2,1)} %bitcast.46) | data formatting | bytes 7340032 | tf_op jit(solution)/shard_map/tec,ehcf->thf/dot_general | solution.py:65
  262.2 3.6 %fusion = bf16[128,3584]{1,0:T(8,128)(2,1)} fusion(bf16[128,8,64]{0,2,1:T(8,128)(2,1)S(1)} %bitcast.53, bf16[3584,64,8]{0,1,2:T(8,128)(2,1)} %dot_general.24), kind=kOutput, calls=%fused_computation.3 | convolution fusion | flops 470220800 | bytes 4718592 | tf_op jit(solution)/shard_map/tec,ehcf->thf/dot_general | solution.py:65
  (10 shorter events, 0.1 us)
Async XLA Ops:
  6.5 118.0 %all-gather.3.cloned.1.call-start = ((), (), s32[]{:S(2)}) async-start(), calls=%async_computation.3 | async-start | bytes 6291456 | tf_op jit(solution)/shard_map/all_gather | solution.py:48
  15.6 89.4 %copy-start.1 = (bf16[1,1792,1024]{2,1,0:T(8,128)(2,1)S(1)}, bf16[1,1792,1024]{2,1,0:T(8,128)(2,1)}, u32[]{:S(2)}) copy-start(bf16[1,1792,1024]{2,1,0:T(8,128)(2,1)} %param.10) | copy-start | bytes 11010052
  103.2 1.8 copy-start
  110.2 39.2 %all-reduce.2.cloned.1.call-start = ((), (), s32[]{:S(2)}) async-start(), calls=%async_computation.2 | async-start | bytes 4194304 | tf_op jit(solution)/shard_map/psum | solution.py:52
  158.6 87.1 %all-to-all-start.1 = ((bf16[16,64,1792]{2,1,0:T(8,128)(2,1)}), bf16[16,64,1792]{2,1,0:T(8,128)(2,1)}, u32[]{:S(2)}, u32[]{:S(2)}) async-start(bf16[16,64,1792]{2,1,0:T(8,128)(2,1)} %bitcast.51), calls=%async_computation.1 | async-start | bytes 7340032 | tf_op jit(solution)/shard_map/all_to_all | solution.py:58
Sparse Core Ops, SparseCore 0:
  110.3 14.1 all-gather.2
  126.8 22.4 all-reduce.1
